TPU v7x, 32 devices: a whole 2x2x4 slice. The times are simulated.
32 devices in a mesh: patch: 2 (over y), tile: 8 (over z, core), row: 2 (over x), band: 1.
Axes of the slice: x: 2, y: 2, z: 4, core: 2. Of those that a mesh axis runs over, the one named last changes fastest.
Arguments:
- stamps: bfloat16 [768, 64, 128], P(('patch', 'tile', 'row', 'band')), parts along dimension 0, may hold values from -6 to 6
- variance: bfloat16 [768, 64, 128], P(('patch', 'tile', 'row', 'band')), parts along dimension 0, may hold values from 0.25 to 4
- basis_v: bfloat16 [21, 41], replicated, may hold values from -1 to 1
- basis_u: bfloat16 [21, 41], replicated, may hold values from -1 to 1
- coefficients: float32 [800, 21], P('patch'), parts along dimension 0, may hold values from 0.03 to 0.3
- coef_index: int32 [768], P(('patch', 'tile', 'row', 'band')), parts along dimension 0, may hold values from 0 to 399
- tile_dest: int32 [768], P(('patch', 'tile', 'row', 'band')), parts along dimension 0, may hold values from 0 to 7, as said below
- row_offset: int32 [768], P(('patch', 'tile', 'row', 'band')), parts along dimension 0, may hold values from 0 to 448
- sub_pixel: int32 [768, 2], P(('patch', 'tile', 'row', 'band')), parts along dimension 0, may hold values from 0 to 63
Outputs:
- coadd: float32 [8192, 128], P(('patch', 'tile', 'row', 'band')), parts along dimension 0
There are 2 independent parts, one for each index of `patch`. A program takes and returns all parts, laid end to end along the dimension named above; an argument that names none is the same for every part. Nothing has to cross between parts.
Inputs may be any that keep to these rules, and one draw needn't show every extreme that they name: `tile_dest`: among the 24 stamps of one device at most 3 name the same tile, and one tile is named by exactly 3 stamps of every device.
All inputs are finite; a program needn't handle non-finite values.
Results may differ from a plain program's by a relative error of at most 0.0055.
Values may be sent and summed in bfloat16 or wider, within the bound.
No kernel may reach another device: no remote copies, remote signals or barrier semaphores. Data moves between devices by JAX's collectives and lax.ppermute only.
A program may use at most 64 MiB of HBM per device.

v0:
```python
import math
import jax
import jax.numpy as jnp
from jax import lax
from jax.sharding import PartitionSpec as P

SUBSTEPS = 64
TILE_ROWS = 512


def band_tables(basis_v, basis_u, stamp_rows, stamp_cols):
    tap_count = basis_v.shape[1]
    half_width = (tap_count - 1) // 2
    row_ids = jnp.arange(stamp_rows)
    col_ids = jnp.arange(stamp_cols)
    tap_ids = jnp.arange(tap_count)
    lag_rows = row_ids[None, :] - row_ids[:, None] + half_width
    pick_rows = (lag_rows[None, :, :] == tap_ids[:, None, None]).astype(jnp.bfloat16)
    vertical = jnp.einsum(
        "ka,aij->kij", basis_v, pick_rows, preferred_element_type=jnp.float32
    ).astype(jnp.bfloat16)
    lag_cols = col_ids[:, None] - col_ids[None, :] + half_width
    pick_cols = (lag_cols[None, :, :] == tap_ids[:, None, None]).astype(jnp.bfloat16)
    horizontal = jnp.einsum(
        "ka,apq->pkq", basis_u, pick_cols, preferred_element_type=jnp.float32
    ).astype(jnp.bfloat16)
    return (vertical, horizontal.reshape(stamp_cols, -1))


def coef_rows(coefficients, indices):
    picks = (indices[:, None] == jnp.arange(coefficients.shape[0])[None, :]).astype(jnp.float32)
    return jnp.dot(picks, coefficients, precision=lax.Precision.HIGHEST)


def match_stamps(images, coef_part, vertical, horiz_table):
    slot_count, stamp_rows, stamp_cols = images.shape
    nbasis = vertical.shape[0]
    group_size = math.gcd(slot_count, 4)

    def one_group(operands):
        group_images, group_coef = operands
        flattened = group_images.reshape(group_size * stamp_rows, stamp_cols)
        horizontal = jnp.dot(flattened, horiz_table, preferred_element_type=jnp.float32).astype(
            jnp.bfloat16
        )
        horizontal = horizontal.reshape(group_size, stamp_rows, nbasis, stamp_cols)
        vertical_out = jnp.einsum(
            "kai,bikc->bkac", vertical, horizontal, preferred_element_type=jnp.float32
        )
        combined = jnp.sum(group_coef[:, :, None, None] * vertical_out, axis=1)
        return combined.astype(jnp.bfloat16)

    grouped = (
        images.reshape(slot_count // group_size, group_size, stamp_rows, stamp_cols),
        coef_part.reshape(slot_count // group_size, group_size, nbasis),
    )
    return lax.map(one_group, grouped).reshape(slot_count, stamp_rows, stamp_cols)


def bilinear(values, frac_rows, frac_cols):
    below = jnp.concatenate([values[:, 1:], values[:, -1:]], axis=1)
    mixed = (1.0 - frac_rows) * values + frac_rows * below
    beside = jnp.concatenate([mixed[:, :, 1:], mixed[:, :, -1:]], axis=2)
    return (1.0 - frac_cols) * mixed + frac_cols * beside


def contributions(matched, spreads, details):
    live = (details[:, 0] > 0)[:, None, None]
    frac_rows = details[:, 2].astype(jnp.float32)[:, None, None] / SUBSTEPS
    frac_cols = details[:, 3].astype(jnp.float32)[:, None, None] / SUBSTEPS
    warped = bilinear(matched.astype(jnp.float32), frac_rows, frac_cols)
    spread = bilinear(spreads.astype(jnp.float32), frac_rows, frac_cols)
    weight = jnp.where(live, 1.0 / jnp.where(live, spread, 1.0), 0.0)
    rows_at = details[:, 1][:, None] + jnp.arange(matched.shape[1], dtype=jnp.int32)[None, :]
    return (weight * warped, weight, rows_at)


def local(
    stamps, variance, basis_v, basis_u, coefficients, coef_index, tile_dest, row_offset, sub_pixel
):
    tile_count = lax.axis_size("tile")
    local_count, stamp_rows, stamp_cols = stamps.shape
    capacity = max(2, (local_count + tile_count - 1) // tile_count)
    slot_total = tile_count * capacity
    vertical, horiz_table = band_tables(basis_v, basis_u, stamp_rows, stamp_cols)
    chosen = (tile_dest[:, None] == jnp.arange(tile_count, dtype=jnp.int32)[None, :]).astype(
        jnp.int32
    )
    earlier = jnp.cumsum(chosen, axis=0) - chosen
    ranking = jnp.sum(earlier * chosen, axis=1)
    slot_of = tile_dest * capacity + ranking

    def pack(values):
        empty_buffer = jnp.zeros((slot_total,) + values.shape[1:], values.dtype)
        filled = empty_buffer.at[slot_of].set(values)
        return filled.reshape((tile_count, capacity) + values.shape[1:])

    base_meta = [jnp.ones_like(row_offset), row_offset, sub_pixel[:, 0], sub_pixel[:, 1]]
    matched_here = match_stamps(stamps, coef_rows(coefficients, coef_index), vertical, horiz_table)
    meta_sent = jnp.stack(base_meta, axis=1)
    images = lax.all_to_all(pack(matched_here), "tile", split_axis=0, concat_axis=0, tiled=True)
    spreads = lax.all_to_all(pack(variance), "tile", split_axis=0, concat_axis=0, tiled=True)
    details = lax.all_to_all(pack(meta_sent), "tile", split_axis=0, concat_axis=0, tiled=True)
    leading = images.shape[:2]
    results = contributions(
        images.reshape((-1,) + images.shape[2:]),
        spreads.reshape((-1,) + spreads.shape[2:]),
        details.reshape(-1, details.shape[2]),
    )
    numer, denom, rows_at = tuple((item.reshape(leading + item.shape[1:]) for item in results))
    rows_flat = rows_at.reshape(-1)
    numer_tile = (
        jnp.zeros((TILE_ROWS, stamp_cols), jnp.float32)
        .at[rows_flat]
        .add(numer.reshape(-1, stamp_cols))
    )
    denom_tile = (
        jnp.zeros((TILE_ROWS, stamp_cols), jnp.float32)
        .at[rows_flat]
        .add(denom.reshape(-1, stamp_cols))
    )
    numer_own, denom_own = (
        lax.psum_scatter(numer_tile, ("row", "band"), scatter_dimension=0, tiled=True),
        lax.psum_scatter(denom_tile, ("row", "band"), scatter_dimension=0, tiled=True),
    )
    return numer_own / (denom_own + 1.0)


def solution(mesh):
    in_specs = (
        P(("patch", "tile", "row", "band"), None, None),
        P(("patch", "tile", "row", "band"), None, None),
        P(),
        P(),
        P("patch", None),
        P(("patch", "tile", "row", "band")),
        P(("patch", "tile", "row", "band")),
        P(("patch", "tile", "row", "band")),
        P(("patch", "tile", "row", "band"), None),
    )
    out_specs = P(("patch", "tile", "row", "band"), None)
    return jax.shard_map(local, mesh=mesh, in_specs=in_specs, out_specs=out_specs, check_vma=False)
```

profile of v0, /device:TPU:0, one launch (start us, length us, event | category | flops | bytes accessed | tf_op | source)
XLA Modules:
  0.0 139.1 jit_solution(17910034526923628088)
XLA Ops:
  6.5 0.7 fusion.31
  7.3 0.8 select_reduce_fusion
  8.8 0.8 pad_add_fusion
  10.3 0.7 copy.32
  11.1 6.4 %all-to-all-start = ((s32[8,3,4]{1,2,0:T(4,128)}), s32[8,3,4]{1,2,0:T(4,128)S(1)}, u32[]{:S(2)}, u32[]{:S(2)}) async-start(s32[8,3,4]{1,2,0:T(4,128)} %copy.32), calls=%async_computation | async-start | bytes 32768 | tf_op jit(solution)/shard_map/all_to_all | solution.py:103
  17.5 1.4 %fusion.7 = bf16[128,21,128]{2,1,0:T(8,128)(2,1)S(1)} fusion(s32[128,128]{1,0:T(8,128)S(1)} %subtract_add_fusion, bf16[21,41]{1,0:T(8,128)(2,1)} %param.14), kind=kOutput, calls=%fused_computation.19 | convolution fusion | flops 29229056 | bytes 755386 | tf_op jit(solution)/shard_map/ka,apq->pkq/dot_general | solution.py:24
  19.4 1.1 copy.36
  20.9 0.8 copy.37
  22.0 30.3 %while.10 = (s32[]{:T(128)}, bf16[6,4,64,128]{3,2,1,0:T(8,128)(2,1)S(1)}, f32[6,4,21]{2,1,0:T(4,128)S(1)}, bf16[6,4,64,128]{3,2,1,0:T(8,128)(2,1)}, bf16[128,268...) while((s32[]{:T(128)}, bf16[6,4,64,128]{3,2,1,0:T(8,128)(2,1)S(1)}, f32[6,4,21]{2,1,0:T(4,128)S(1)}, ...), condition=%wide.region_6.7_spmd, body=%wide.region_4.6_spmd.sunk | while | flops 266272768 | bytes 6760169 | solution.py:57
  22.0 0.8 constant_dynamic-slice_fusion.2
  22.8 1.6 %convolution_convert_fusion.2 = bf16[256,2688]{1,0:T(8,128)(2,1)S(1)} fusion(bf16[256,128]{1,0:T(8,128)(2,1)S(1)} %bitcast.99, bf16[128,2688]{1,0:T(8,128)(2,1)} %get-tuple-element.135), kind=kOutput, calls=%fused_computation.5.clone.1 | convolution fusion | flops 176848896 | bytes 2129920 | tf_op jit(solution)/shard_map/while/body/eval_jaxpr/dot_general | solution.py:43
  24.5 0.9 reshape.241
  25.5 1.5 %fusion.49 = bf16[4,64,128]{2,1,0:T(8,128)(2,1)S(1)} fusion(bf16[4,64,21,128]{3,2,1,0:T(8,128)(2,1)S(1)} %reshape.241, f32[4,21]{0,1:T(8,128)S(1)} %copy.47, bf16[21,64,64]{2,1,0:T(8,128)(2,1)} %get-tuple-element.136), kind=kOutput, calls=%fused_computation.7.clone.1 | convolution fusion | flops 89423872 | bytes 1614160 | tf_op jit(solution)/shard_map/while/body/eval_jaxpr/kai,bikc->bkac/dot_general | solution.py:47
  27.0 0.8 constant_dynamic-slice_fusion.2
  27.9 1.6 %convolution_convert_fusion.2 = bf16[256,2688]{1,0:T(8,128)(2,1)S(1)} fusion(bf16[256,128]{1,0:T(8,128)(2,1)S(1)} %bitcast.99, bf16[128,2688]{1,0:T(8,128)(2,1)} %get-tuple-element.135), kind=kOutput, calls=%fused_computation.5.clone.1 | convolution fusion | flops 176848896 | bytes 2129920 | tf_op jit(solution)/shard_map/while/body/eval_jaxpr/dot_general | solution.py:43
  29.5 0.9 reshape.241
  30.6 1.5 %fusion.49 = bf16[4,64,128]{2,1,0:T(8,128)(2,1)S(1)} fusion(bf16[4,64,21,128]{3,2,1,0:T(8,128)(2,1)S(1)} %reshape.241, f32[4,21]{0,1:T(8,128)S(1)} %copy.47, bf16[21,64,64]{2,1,0:T(8,128)(2,1)} %get-tuple-element.136), kind=kOutput, calls=%fused_computation.7.clone.1 | convolution fusion | flops 89423872 | bytes 1614160 | tf_op jit(solution)/shard_map/while/body/eval_jaxpr/kai,bikc->bkac/dot_general | solution.py:47
  32.1 0.8 constant_dynamic-slice_fusion.2
  32.9 1.6 %convolution_convert_fusion.2 = bf16[256,2688]{1,0:T(8,128)(2,1)S(1)} fusion(bf16[256,128]{1,0:T(8,128)(2,1)S(1)} %bitcast.99, bf16[128,2688]{1,0:T(8,128)(2,1)} %get-tuple-element.135), kind=kOutput, calls=%fused_computation.5.clone.1 | convolution fusion | flops 176848896 | bytes 2129920 | tf_op jit(solution)/shard_map/while/body/eval_jaxpr/dot_general | solution.py:43
  34.6 0.9 reshape.241
  35.6 1.5 %fusion.49 = bf16[4,64,128]{2,1,0:T(8,128)(2,1)S(1)} fusion(bf16[4,64,21,128]{3,2,1,0:T(8,128)(2,1)S(1)} %reshape.241, f32[4,21]{0,1:T(8,128)S(1)} %copy.47, bf16[21,64,64]{2,1,0:T(8,128)(2,1)} %get-tuple-element.136), kind=kOutput, calls=%fused_computation.7.clone.1 | convolution fusion | flops 89423872 | bytes 1614160 | tf_op jit(solution)/shard_map/while/body/eval_jaxpr/kai,bikc->bkac/dot_general | solution.py:47
  37.1 0.8 constant_dynamic-slice_fusion.2
  38.0 1.6 %convolution_convert_fusion.2 = bf16[256,2688]{1,0:T(8,128)(2,1)S(1)} fusion(bf16[256,128]{1,0:T(8,128)(2,1)S(1)} %bitcast.99, bf16[128,2688]{1,0:T(8,128)(2,1)} %get-tuple-element.135), kind=kOutput, calls=%fused_computation.5.clone.1 | convolution fusion | flops 176848896 | bytes 2129920 | tf_op jit(solution)/shard_map/while/body/eval_jaxpr/dot_general | solution.py:43
  39.6 0.9 reshape.241
  40.6 1.5 %fusion.49 = bf16[4,64,128]{2,1,0:T(8,128)(2,1)S(1)} fusion(bf16[4,64,21,128]{3,2,1,0:T(8,128)(2,1)S(1)} %reshape.241, f32[4,21]{0,1:T(8,128)S(1)} %copy.47, bf16[21,64,64]{2,1,0:T(8,128)(2,1)} %get-tuple-element.136), kind=kOutput, calls=%fused_computation.7.clone.1 | convolution fusion | flops 89423872 | bytes 1614160 | tf_op jit(solution)/shard_map/while/body/eval_jaxpr/kai,bikc->bkac/dot_general | solution.py:47
  42.2 0.8 constant_dynamic-slice_fusion.2
  43.0 1.6 %convolution_convert_fusion.2 = bf16[256,2688]{1,0:T(8,128)(2,1)S(1)} fusion(bf16[256,128]{1,0:T(8,128)(2,1)S(1)} %bitcast.99, bf16[128,2688]{1,0:T(8,128)(2,1)} %get-tuple-element.135), kind=kOutput, calls=%fused_computation.5.clone.1 | convolution fusion | flops 176848896 | bytes 2129920 | tf_op jit(solution)/shard_map/while/body/eval_jaxpr/dot_general | solution.py:43
  44.7 0.9 reshape.241
  45.7 1.5 %fusion.49 = bf16[4,64,128]{2,1,0:T(8,128)(2,1)S(1)} fusion(bf16[4,64,21,128]{3,2,1,0:T(8,128)(2,1)S(1)} %reshape.241, f32[4,21]{0,1:T(8,128)S(1)} %copy.47, bf16[21,64,64]{2,1,0:T(8,128)(2,1)} %get-tuple-element.136), kind=kOutput, calls=%fused_computation.7.clone.1 | convolution fusion | flops 89423872 | bytes 1614160 | tf_op jit(solution)/shard_map/while/body/eval_jaxpr/kai,bikc->bkac/dot_general | solution.py:47
  47.2 0.8 constant_dynamic-slice_fusion.2
  48.1 1.6 %convolution_convert_fusion.2 = bf16[256,2688]{1,0:T(8,128)(2,1)S(1)} fusion(bf16[256,128]{1,0:T(8,128)(2,1)S(1)} %bitcast.99, bf16[128,2688]{1,0:T(8,128)(2,1)} %get-tuple-element.135), kind=kOutput, calls=%fused_computation.5.clone.1 | convolution fusion | flops 176848896 | bytes 2129920 | tf_op jit(solution)/shard_map/while/body/eval_jaxpr/dot_general | solution.py:43
  49.7 0.9 reshape.241
  50.7 1.5 %fusion.49 = bf16[4,64,128]{2,1,0:T(8,128)(2,1)S(1)} fusion(bf16[4,64,21,128]{3,2,1,0:T(8,128)(2,1)S(1)} %reshape.241, f32[4,21]{0,1:T(8,128)S(1)} %copy.47, bf16[21,64,64]{2,1,0:T(8,128)(2,1)} %get-tuple-element.136), kind=kOutput, calls=%fused_computation.7.clone.1 | convolution fusion | flops 89423872 | bytes 1614160 | tf_op jit(solution)/shard_map/while/body/eval_jaxpr/kai,bikc->bkac/dot_general | solution.py:47
  52.3 0.8 broadcast.157.clone
  53.1 4.4 %scatter_fusion.1 = bf16[24,64,128]{2,1,0:T(8,128)(2,1)} fusion(bf16[24,64,128]{2,1,0:T(8,128)(2,1)} %broadcast.157.clone, s32[24]{0:T(128)S(1)} %compare_select_fusion.1, bf16[24,64,128]{2,1,0:T(8,128)(2,1)S(1)} %bitcast.105), kind=kCustom, calls=%fused_computation.2 | custom fusion | bytes 1179744 | tf_op jit(solution)/shard_map/scatter | solution.py:95
  57.5 5.1 %all-to-all-start.2 = ((bf16[8,3,64,128]{3,2,1,0:T(8,128)(2,1)}), bf16[8,3,64,128]{3,2,1,0:T(8,128)(2,1)S(1)}, u32[]{:S(2)}, u32[]{:S(2)}) async-start(bf16[8,3,64,128]{3,2,1,0:T(8,128)(2,1)} %bitcast.25), calls=%async_computation.2 | async-start | bytes 786432 | tf_op jit(solution)/shard_map/all_to_all | solution.py:101
  62.6 0.8 broadcast.157.clone.1
  63.4 4.4 %scatter_fusion = bf16[24,64,128]{2,1,0:T(8,128)(2,1)} fusion(bf16[24,64,128]{2,1,0:T(8,128)(2,1)} %broadcast.157.clone.1, s32[24]{0:T(128)S(1)} %compare_select_fusion.1, bf16[24,64,128]{2,1,0:T(8,128)(2,1)S(1)} %copy-done.1), kind=kCustom, calls=%fused_computation.1 | custom fusion | bytes 1179744 | tf_op jit(solution)/shard_map/scatter | solution.py:95
  68.4 6.6 %all-to-all-done.2 = bf16[8,3,64,128]{3,2,1,0:T(8,128)(2,1)S(1)} async-done(((bf16[8,3,64,128]{3,2,1,0:T(8,128)(2,1)}), bf16[8,3,64,128]{3,2,1,0:T(8,128)(2,1)S(1)}, u32[]{:S(2)}, u32[]{:S(2)}) %all-to-all-start.2) | async-done | bytes 393248 | tf_op jit(solution)/shard_map/all_to_all | solution.py:101
  75.1 3.5 %all-to-all-start.1 = ((bf16[8,3,64,128]{3,2,1,0:T(8,128)(2,1)}), bf16[8,3,64,128]{3,2,1,0:T(8,128)(2,1)S(1)}, u32[]{:S(2)}, u32[]{:S(2)}) async-start(bf16[8,3,64,128]{3,2,1,0:T(8,128)(2,1)} %bitcast.11), calls=%async_computation.1 | async-start | bytes 786432 | tf_op jit(solution)/shard_map/all_to_all | solution.py:102
  79.1 11.9 %all-to-all-done.1 = bf16[8,3,64,128]{3,2,1,0:T(8,128)(2,1)S(1)} async-done(((bf16[8,3,64,128]{3,2,1,0:T(8,128)(2,1)}), bf16[8,3,64,128]{3,2,1,0:T(8,128)(2,1)S(1)}, u32[]{:S(2)}, u32[]{:S(2)}) %all-to-all-start.1) | async-done | bytes 393248 | tf_op jit(solution)/shard_map/all_to_all | solution.py:102
  92.3 1.2 slice.58
  93.4 1.7 %fusion.21 = (f32[1536,128]{1,0:T(8,128)S(1)}, f32[1536,128]{1,0:T(8,128)S(1)}) fusion(f32[24,64,128]{2,1,0:T(8,128)S(1)} %get-tuple-element.69, f32[1536]{0:T(1024)S(1)} %mul.126, f32[1536]{0:T(1024)S(1)} %mul.122, f32[1536]{0:T(1024)S(1)} %mul.119, bf16[8,3,64,128]{3,2,1,0:T(8,128)(2,1)S(1)} %all-to-all-done.2, f32[1536,1]{1,0:T(8,128)S(1)} %bitcast.101, ...), kind=kLoop, calls=%fused_computation.37 | loop fusion | flops 3145728 | bytes 4744704 | tf_op jit(solution)/shard_map/mul | solution.py:64
  95.1 10.6 %scatter_custom_fusion.3 = f32[512,128]{1,0:T(8,128)} fusion(s32[1536]{0:T(1024)S(1)} %fusion.32, f32[1536,128]{1,0:T(8,128)S(1)} %get-tuple-element.73, f32[1536,128]{1,0:T(8,128)S(1)} %get-tuple-element.72, f32[1536,1]{1,0:T(8,128)} %bitcast.103, f32[]{:T(128)} %constant.55, f32[1536,127]{1,0:T(8,128)S(1)} %bitcast.102, f32[1536]{0:T(1024)S(1)} %mul.131, ...), kind=kCustom, calls=%fused_computation.32 | custom fusion | flops 983040 | bytes 2635784 | tf_op jit(solution)/shard_map/scatter-add | solution.py:115
  105.8 9.4 %scatter_custom_fusion.4 = f32[512,128]{1,0:T(8,128)} fusion(s32[1536]{0:T(1024)S(1)} %fusion.32, f32[1536,128]{1,0:T(8,128)S(1)} %get-tuple-element.73, f32[]{:T(128)} %constant.18.clone.1), kind=kCustom, calls=%fused_computation.48 | custom fusion | flops 196608 | bytes 262148 | tf_op jit(solution)/shard_map/scatter-add | solution.py:120
  115.2 1.4 reduce-scatter.3.cloned.1.call-done
  116.6 14.0 %reduce-scatter.5.cloned.1.call-done = f32[256,128]{1,0:T(8,128)} async-done(((f32[512,128]{1,0:T(8,128)}), f32[256,128]{1,0:T(8,128)}) %reduce-scatter.5.cloned.1.call-update) | async-done | bytes 131088 | tf_op jit(solution)/shard_map/reduce_scatter | solution.py:124
  130.6 1.6 %add_divide_fusion = f32[256,128]{1,0:T(8,128)} fusion(f32[256,128]{1,0:T(8,128)} %reduce-scatter.3.cloned.1.call-done, f32[256,128]{1,0:T(8,128)} %reduce-scatter.5.cloned.1.call-done), kind=kLoop, calls=%fused_computation.47 | loop fusion | flops 65536 | bytes 393216 | tf_op jit(solution)/shard_map/div | solution.py:126
  (70 shorter events, 5.9 us)
Async XLA Ops:
  6.5 15.2 %copy-start = (f32[400,21]{0,1:T(8,128)S(1)}, f32[400,21]{0,1:T(8,128)}, u32[]{:S(2)}) copy-start(f32[400,21]{0,1:T(8,128)} %param.15) | copy-start | bytes 100804
  11.1 46.4 %all-to-all-start = ((s32[8,3,4]{1,2,0:T(4,128)}), s32[8,3,4]{1,2,0:T(4,128)S(1)}, u32[]{:S(2)}, u32[]{:S(2)}) async-start(s32[8,3,4]{1,2,0:T(4,128)} %copy.32), calls=%async_computation | async-start | bytes 32768 | tf_op jit(solution)/shard_map/all_to_all | solution.py:103
  18.9 1.7 %copy-start.2 = (bf16[21,41]{1,0:T(8,128)(2,1)S(1)}, bf16[21,41]{1,0:T(8,128)(2,1)}, u32[]{:S(2)}) copy-start(bf16[21,41]{1,0:T(8,128)(2,1)} %param.13) | copy-start | bytes 5170
  19.4 2.4 %copy-start.3 = (s32[24]{0:T(128)S(1)}, s32[24]{0:T(128)}, u32[]{:S(2)}) copy-start(s32[24]{0:T(128)} %param.16) | copy-start | bytes 292
  52.3 11.1 %copy-start.1 = (bf16[24,64,128]{2,1,0:T(8,128)(2,1)S(1)}, bf16[24,64,128]{2,1,0:T(8,128)(2,1)}, u32[]{:S(2)}) copy-start(bf16[24,64,128]{2,1,0:T(8,128)(2,1)} %param.12) | copy-start | bytes 1179652
  57.5 17.6 %all-to-all-start.2 = ((bf16[8,3,64,128]{3,2,1,0:T(8,128)(2,1)}), bf16[8,3,64,128]{3,2,1,0:T(8,128)(2,1)S(1)}, u32[]{:S(2)}, u32[]{:S(2)}) async-start(bf16[8,3,64,128]{3,2,1,0:T(8,128)(2,1)} %bitcast.25), calls=%async_computation.2 | async-start | bytes 786432 | tf_op jit(solution)/shard_map/all_to_all | solution.py:101
  75.1 15.9 %all-to-all-start.1 = ((bf16[8,3,64,128]{3,2,1,0:T(8,128)(2,1)}), bf16[8,3,64,128]{3,2,1,0:T(8,128)(2,1)S(1)}, u32[]{:S(2)}, u32[]{:S(2)}) async-start(bf16[8,3,64,128]{3,2,1,0:T(8,128)(2,1)} %bitcast.11), calls=%async_computation.1 | async-start | bytes 786432 | tf_op jit(solution)/shard_map/all_to_all | solution.py:102
  78.5 38.1 %reduce-scatter.3.cloned.1.call-start = ((), (), s32[]{:S(2)}) async-start(), calls=%async_computation.5 | async-start | bytes 393216 | tf_op jit(solution)/shard_map/reduce_scatter | solution.py:123
  105.8 24.9 %reduce-scatter.5.cloned.1.call-start = ((), (), s32[]{:S(2)}) async-start(), calls=%async_computation.6 | async-start | bytes 393216 | tf_op jit(solution)/shard_map/reduce_scatter | solution.py:124
Sparse Core Ops, SparseCore 0:
  105.9 10.6 reduce-scatter.2
  118.8 11.7 reduce-scatter.4
where the time goes:
time: 141 us; the launch traced here: 139 us
  waiting for transfers between devices  34 us (24%)
  local copies, waits for them, and re-layouts  28.8 us (20%)
  other arithmetic  26.9 us (19%)
  matrix products  20.6 us (15%)
  starting transfers between devices  15 us (11%)
  between operations  13.6 us (10%)
    reduce_scatter x1, waiting for transfers between devices, local(): lax.psum_scatter(denom_tile, ('row', 'band'), scatter_dimension=0, tiled=...  14 us
    all_to_all x1, waiting for transfers between devices, local(): lax.all_to_all(pack(variance), 'tile', split_axis=0, concat_axis=0, tiled...  11.9 us
    scatter-add x1, other arithmetic, local(): numer_tile = jnp.zeros((TILE_ROWS, stamp_cols), jnp.float32).at[rows_flat...  10.6 us
    dot_general x6, matrix products, one_group(): jnp.dot(flattened, horiz_table, preferred_element_type=jnp.float32)  9.64 us
    scatter-add x1, other arithmetic, local(): denom_tile = jnp.zeros((TILE_ROWS, stamp_cols), jnp.float32).at[rows_flat...  9.4 us
    scatter x3, local copies, waits for them, and re-layouts, pack(): filled = empty_buffer.at[slot_of].set(values)  9.37 us
    dot_general x6, matrix products, one_group(): jnp.einsum('kai,bikc->bkac', vertical, horizontal, preferred_element_type...  8.99 us
    all_to_all x1, waiting for transfers between devices, local(): lax.all_to_all(pack(matched_here), 'tile', split_axis=0, concat_axis=0, t...  6.64 us
  transfers between devices with their start and end apart: 5, of which 4 were waited for; matrix products, arithmetic and copies ran while one was open for 40% of the time, Pallas kernels for 0%

commit v1 on v0

--- a/solution.py
+++ b/solution.py
@@ -6,6 +6,29 @@
 
 SUBSTEPS = 64
 TILE_ROWS = 512
+
+
+def in_blocks(x, dim, peers):
+    lengths = x.shape
+    parts = x.reshape(*lengths[:dim], peers, lengths[dim] // peers, *lengths[dim + 1 :])
+    return jnp.moveaxis(parts, dim, 0)
+
+
+def in_order(parts, dim):
+    parts = jnp.moveaxis(parts, 0, dim)
+    shape = parts.shape
+    return parts.reshape(*shape[:dim], shape[dim] * shape[dim + 1], *shape[dim + 2 :])
+
+
+def exchange_in_pairs(x, axis, split_dim, concat_dim):
+    size, position = (lax.axis_size(axis), lax.axis_index(axis))
+    parts = in_blocks(x, split_dim, size)
+    gathered = [parts[position]]
+    for lap in range(1, size):
+        sent = parts[position ^ lap]
+        gathered.append(lax.ppermute(sent, axis, [(i, i ^ lap) for i in range(size)]))
+    parts = jnp.stack(gathered)[position ^ jnp.arange(size)]
+    return in_order(parts, concat_dim)
 
 
 def band_tables(basis_v, basis_u, stamp_rows, stamp_cols):
@@ -98,7 +121,7 @@
     base_meta = [jnp.ones_like(row_offset), row_offset, sub_pixel[:, 0], sub_pixel[:, 1]]
     matched_here = match_stamps(stamps, coef_rows(coefficients, coef_index), vertical, horiz_table)
     meta_sent = jnp.stack(base_meta, axis=1)
-    images = lax.all_to_all(pack(matched_here), "tile", split_axis=0, concat_axis=0, tiled=True)
+    images = exchange_in_pairs(pack(matched_here), "tile", 0, 0)
     spreads = lax.all_to_all(pack(variance), "tile", split_axis=0, concat_axis=0, tiled=True)
     details = lax.all_to_all(pack(meta_sent), "tile", split_axis=0, concat_axis=0, tiled=True)
     leading = images.shape[:2]

time: 141 us -> 134 us (0.950)
  waiting for transfers between devices: 34 us -> 26.5 us
  starting transfers between devices: 15 us -> 19.5 us
  local copies, waits for them, and re-layouts: 28.8 us -> 26 us
    all_to_all x1, waiting for transfers between devices: 11.9 us -> 1.36 us  [local(): lax.all_to_all(pack(variance), 'tile', split_axis=0, concat_axis=0, tiled...]
    ppermute x0 -> x7, starting transfers between devices: none -> 9.89 us  [exchange_in_pairs(): lax.ppermute(sent, axis, [(i, i ^ lap) for i in range(size)])]
    ppermute x0 -> x7, waiting for transfers between devices: none -> 7.91 us  [exchange_in_pairs(): lax.ppermute(sent, axis, [(i, i ^ lap) for i in range(size)])]
    all_to_all x1 -> x0, waiting for transfers between devices: 6.64 us -> none  [local(): lax.all_to_all(pack(matched_here), 'tile', split_axis=0, concat_axis=0, t...]
    all_to_all x1 -> x0, starting transfers between devices: 5.07 us -> none  [local(): lax.all_to_all(pack(matched_here), 'tile', split_axis=0, concat_axis=0, t...]
    scatter x3, local copies, waits for them, and re-layouts: 9.37 us -> 6.6 us  [pack(): filled = empty_buffer.at[slot_of].set(values)]
    all_to_all x1, starting transfers between devices: 6.35 us -> 4.92 us  [local(): lax.all_to_all(pack(meta_sent), 'tile', split_axis=0, concat_axis=0, tile...]
  transfers between devices with their start and end apart: 5 -> 11, of which waited for: 4 -> 5; matrix products, arithmetic and copies ran while one was open for 40% -> 14% of each run, Pallas kernels for 0% -> 0%
where the time goes in v1:
time: 134 us; the launch traced here: 133 us
  waiting for transfers between devices  26.5 us (20%)
  other arithmetic  26.2 us (20%)
  local copies, waits for them, and re-layouts  26 us (19%)
  matrix products  20.6 us (15%)
  starting transfers between devices  19.5 us (15%)
  between operations  13.8 us (10%)
    reduce_scatter x1, waiting for transfers between devices, local(): lax.psum_scatter(denom_tile, ('row', 'band'), scatter_dimension=0, tiled=...  14 us
    scatter-add x1, other arithmetic, local(): numer_tile = jnp.zeros((TILE_ROWS, stamp_cols), jnp.float32).at[rows_flat...  10.6 us
    ppermute x7, starting transfers between devices, exchange_in_pairs(): lax.ppermute(sent, axis, [(i, i ^ lap) for i in range(size)])  9.89 us
    dot_general x6, matrix products, one_group(): jnp.dot(flattened, horiz_table, preferred_element_type=jnp.float32)  9.64 us
    scatter-add x1, other arithmetic, local(): denom_tile = jnp.zeros((TILE_ROWS, stamp_cols), jnp.float32).at[rows_flat...  9.4 us
    dot_general x6, matrix products, one_group(): jnp.einsum('kai,bikc->bkac', vertical, horizontal, preferred_element_type...  8.99 us
    ppermute x7, waiting for transfers between devices, exchange_in_pairs(): lax.ppermute(sent, axis, [(i, i ^ lap) for i in range(size)])  7.91 us
    scatter x3, local copies, waits for them, and re-layouts, pack(): filled = empty_buffer.at[slot_of].set(values)  6.6 us
  transfers between devices with their start and end apart: 11, of which 5 were waited for; matrix products, arithmetic and copies ran while one was open for 14% of the time, Pallas kernels for 0%

profile of v1, /device:TPU:0, one launch (start us, length us, event | category | flops | bytes accessed | tf_op | source)
XLA Modules:
  0.0 133.0 jit_solution(18079804288980184456)
XLA Ops:
  6.6 0.7 fusion.31
  7.4 0.8 select_reduce_fusion
  8.9 1.4 %fusion.7 = bf16[128,21,128]{2,1,0:T(8,128)(2,1)S(1)} fusion(s32[128,128]{1,0:T(8,128)S(1)} %subtract_add_fusion, bf16[21,41]{1,0:T(8,128)(2,1)} %param.14), kind=kOutput, calls=%fused_computation.20 | convolution fusion | flops 29229056 | bytes 755386 | tf_op jit(solution)/shard_map/ka,apq->pkq/dot_general | solution.py:47
  10.8 1.1 copy.36
  12.3 0.8 copy.37
  13.4 30.3 %while.10 = (s32[]{:T(128)}, bf16[6,4,64,128]{3,2,1,0:T(8,128)(2,1)S(1)}, f32[6,4,21]{2,1,0:T(4,128)S(1)}, bf16[6,4,64,128]{3,2,1,0:T(8,128)(2,1)}, bf16[128,268...) while((s32[]{:T(128)}, bf16[6,4,64,128]{3,2,1,0:T(8,128)(2,1)S(1)}, f32[6,4,21]{2,1,0:T(4,128)S(1)}, ...), condition=%wide.region_6.7_spmd, body=%wide.region_4.6_spmd.sunk | while | flops 266272768 | bytes 6760169 | solution.py:80
  13.4 0.8 constant_dynamic-slice_fusion.2
  14.2 1.6 %convolution_convert_fusion.2 = bf16[256,2688]{1,0:T(8,128)(2,1)S(1)} fusion(bf16[256,128]{1,0:T(8,128)(2,1)S(1)} %bitcast.130, bf16[128,2688]{1,0:T(8,128)(2,1)} %get-tuple-element.143), kind=kOutput, calls=%fused_computation.6.clone.1 | convolution fusion | flops 176848896 | bytes 2129920 | tf_op jit(solution)/shard_map/while/body/eval_jaxpr/dot_general | solution.py:66
  15.9 0.9 reshape.266
  16.9 1.5 %fusion.50 = bf16[4,64,128]{2,1,0:T(8,128)(2,1)S(1)} fusion(bf16[4,64,21,128]{3,2,1,0:T(8,128)(2,1)S(1)} %reshape.266, f32[4,21]{0,1:T(8,128)S(1)} %copy.47, bf16[21,64,64]{2,1,0:T(8,128)(2,1)} %get-tuple-element.144), kind=kOutput, calls=%fused_computation.8.clone.1 | convolution fusion | flops 89423872 | bytes 1614160 | tf_op jit(solution)/shard_map/while/body/eval_jaxpr/kai,bikc->bkac/dot_general | solution.py:70
  18.4 0.8 constant_dynamic-slice_fusion.2
  19.3 1.6 %convolution_convert_fusion.2 = bf16[256,2688]{1,0:T(8,128)(2,1)S(1)} fusion(bf16[256,128]{1,0:T(8,128)(2,1)S(1)} %bitcast.130, bf16[128,2688]{1,0:T(8,128)(2,1)} %get-tuple-element.143), kind=kOutput, calls=%fused_computation.6.clone.1 | convolution fusion | flops 176848896 | bytes 2129920 | tf_op jit(solution)/shard_map/while/body/eval_jaxpr/dot_general | solution.py:66
  20.9 0.9 reshape.266
  21.9 1.5 %fusion.50 = bf16[4,64,128]{2,1,0:T(8,128)(2,1)S(1)} fusion(bf16[4,64,21,128]{3,2,1,0:T(8,128)(2,1)S(1)} %reshape.266, f32[4,21]{0,1:T(8,128)S(1)} %copy.47, bf16[21,64,64]{2,1,0:T(8,128)(2,1)} %get-tuple-element.144), kind=kOutput, calls=%fused_computation.8.clone.1 | convolution fusion | flops 89423872 | bytes 1614160 | tf_op jit(solution)/shard_map/while/body/eval_jaxpr/kai,bikc->bkac/dot_general | solution.py:70
  23.5 0.8 constant_dynamic-slice_fusion.2
  24.3 1.6 %convolution_convert_fusion.2 = bf16[256,2688]{1,0:T(8,128)(2,1)S(1)} fusion(bf16[256,128]{1,0:T(8,128)(2,1)S(1)} %bitcast.130, bf16[128,2688]{1,0:T(8,128)(2,1)} %get-tuple-element.143), kind=kOutput, calls=%fused_computation.6.clone.1 | convolution fusion | flops 176848896 | bytes 2129920 | tf_op jit(solution)/shard_map/while/body/eval_jaxpr/dot_general | solution.py:66
  26.0 0.9 reshape.266
  27.0 1.5 %fusion.50 = bf16[4,64,128]{2,1,0:T(8,128)(2,1)S(1)} fusion(bf16[4,64,21,128]{3,2,1,0:T(8,128)(2,1)S(1)} %reshape.266, f32[4,21]{0,1:T(8,128)S(1)} %copy.47, bf16[21,64,64]{2,1,0:T(8,128)(2,1)} %get-tuple-element.144), kind=kOutput, calls=%fused_computation.8.clone.1 | convolution fusion | flops 89423872 | bytes 1614160 | tf_op jit(solution)/shard_map/while/body/eval_jaxpr/kai,bikc->bkac/dot_general | solution.py:70
  28.5 0.8 constant_dynamic-slice_fusion.2
  29.4 1.6 %convolution_convert_fusion.2 = bf16[256,2688]{1,0:T(8,128)(2,1)S(1)} fusion(bf16[256,128]{1,0:T(8,128)(2,1)S(1)} %bitcast.130, bf16[128,2688]{1,0:T(8,128)(2,1)} %get-tuple-element.143), kind=kOutput, calls=%fused_computation.6.clone.1 | convolution fusion | flops 176848896 | bytes 2129920 | tf_op jit(solution)/shard_map/while/body/eval_jaxpr/dot_general | solution.py:66
  31.0 0.9 reshape.266
  32.0 1.5 %fusion.50 = bf16[4,64,128]{2,1,0:T(8,128)(2,1)S(1)} fusion(bf16[4,64,21,128]{3,2,1,0:T(8,128)(2,1)S(1)} %reshape.266, f32[4,21]{0,1:T(8,128)S(1)} %copy.47, bf16[21,64,64]{2,1,0:T(8,128)(2,1)} %get-tuple-element.144), kind=kOutput, calls=%fused_computation.8.clone.1 | convolution fusion | flops 89423872 | bytes 1614160 | tf_op jit(solution)/shard_map/while/body/eval_jaxpr/kai,bikc->bkac/dot_general | solution.py:70
  33.6 0.8 constant_dynamic-slice_fusion.2
  34.4 1.6 %convolution_convert_fusion.2 = bf16[256,2688]{1,0:T(8,128)(2,1)S(1)} fusion(bf16[256,128]{1,0:T(8,128)(2,1)S(1)} %bitcast.130, bf16[128,2688]{1,0:T(8,128)(2,1)} %get-tuple-element.143), kind=kOutput, calls=%fused_computation.6.clone.1 | convolution fusion | flops 176848896 | bytes 2129920 | tf_op jit(solution)/shard_map/while/body/eval_jaxpr/dot_general | solution.py:66
  36.0 0.9 reshape.266
  37.1 1.5 %fusion.50 = bf16[4,64,128]{2,1,0:T(8,128)(2,1)S(1)} fusion(bf16[4,64,21,128]{3,2,1,0:T(8,128)(2,1)S(1)} %reshape.266, f32[4,21]{0,1:T(8,128)S(1)} %copy.47, bf16[21,64,64]{2,1,0:T(8,128)(2,1)} %get-tuple-element.144), kind=kOutput, calls=%fused_computation.8.clone.1 | convolution fusion | flops 89423872 | bytes 1614160 | tf_op jit(solution)/shard_map/while/body/eval_jaxpr/kai,bikc->bkac/dot_general | solution.py:70
  38.6 0.8 constant_dynamic-slice_fusion.2
  39.5 1.6 %convolution_convert_fusion.2 = bf16[256,2688]{1,0:T(8,128)(2,1)S(1)} fusion(bf16[256,128]{1,0:T(8,128)(2,1)S(1)} %bitcast.130, bf16[128,2688]{1,0:T(8,128)(2,1)} %get-tuple-element.143), kind=kOutput, calls=%fused_computation.6.clone.1 | convolution fusion | flops 176848896 | bytes 2129920 | tf_op jit(solution)/shard_map/while/body/eval_jaxpr/dot_general | solution.py:66
  41.1 0.9 reshape.266
  42.1 1.5 %fusion.50 = bf16[4,64,128]{2,1,0:T(8,128)(2,1)S(1)} fusion(bf16[4,64,21,128]{3,2,1,0:T(8,128)(2,1)S(1)} %reshape.266, f32[4,21]{0,1:T(8,128)S(1)} %copy.47, bf16[21,64,64]{2,1,0:T(8,128)(2,1)} %get-tuple-element.144), kind=kOutput, calls=%fused_computation.8.clone.1 | convolution fusion | flops 89423872 | bytes 1614160 | tf_op jit(solution)/shard_map/while/body/eval_jaxpr/kai,bikc->bkac/dot_general | solution.py:70
  43.8 1.6 %scatter_fusion.1 = bf16[24,64,128]{2,1,0:T(8,128)(2,1)S(1)} fusion(bf16[24,64,128]{2,1,0:T(8,128)(2,1)S(1)} %broadcast.184.clone, s32[24]{0:T(128)S(1)} %compare_select_fusion.2, bf16[24,64,128]{2,1,0:T(8,128)(2,1)S(1)} %bitcast.138), kind=kCustom, calls=%fused_computation.3 | custom fusion | bytes 1179744 | tf_op jit(solution)/shard_map/scatter | solution.py:118
  46.0 2.6 %collective-permute-start.1 = (bf16[1,3,64,128]{3,2,1,0:T(8,128)(2,1)S(1)}, bf16[1,3,64,128]{3,2,1,0:T(8,128)(2,1)S(1)}, u32[]{:S(2)}, u32[]{:S(2)}) collective-permute-start(bf16[1,3,64,128]{3,2,1,0:T(8,128)(2,1)S(1)} %get-tuple-element.77), channel_id=1, source_target_pairs={{0,4},{2,6},{4,0},{6,2},{8,12},{10,14},{12,8},{14,10},{1,5},{3,7},... | collective-permute-start | bytes 147464 | tf_op jit(solution)/shard_map/ppermute | solution.py:29
  48.7 2.8 %collective-permute-start.3 = (bf16[1,3,64,128]{3,2,1,0:T(8,128)(2,1)S(1)}, bf16[1,3,64,128]{3,2,1,0:T(8,128)(2,1)S(1)}, u32[]{:S(2)}, u32[]{:S(2)}) collective-permute-start(bf16[1,3,64,128]{3,2,1,0:T(8,128)(2,1)S(1)} %get-tuple-element.75), channel_id=1, source_target_pairs={{0,8},{2,10},{4,12},{6,14},{8,0},{10,2},{12,4},{14,6},{1,9},{3,11}... | collective-permute-start | bytes 147464 | tf_op jit(solution)/shard_map/ppermute | solution.py:29
  52.3 0.7 copy.32
  53.1 4.9 %all-to-all-start = ((s32[8,3,4]{1,2,0:T(4,128)}), s32[8,3,4]{1,2,0:T(4,128)S(1)}, u32[]{:S(2)}, u32[]{:S(2)}) async-start(s32[8,3,4]{1,2,0:T(4,128)} %copy.32), calls=%async_computation | async-start | bytes 32768 | tf_op jit(solution)/shard_map/all_to_all | solution.py:126
  58.0 0.8 broadcast.184.clone.1
  58.8 4.4 %scatter_fusion = bf16[24,64,128]{2,1,0:T(8,128)(2,1)} fusion(bf16[24,64,128]{2,1,0:T(8,128)(2,1)} %broadcast.184.clone.1, s32[24]{0:T(128)S(1)} %compare_select_fusion.2, bf16[24,64,128]{2,1,0:T(8,128)(2,1)S(1)} %copy-done.1), kind=kCustom, calls=%fused_computation.2 | custom fusion | bytes 1179744 | tf_op jit(solution)/shard_map/scatter | solution.py:118
  63.6 4.6 %all-to-all-start.1 = ((bf16[8,3,64,128]{3,2,1,0:T(8,128)(2,1)}), bf16[8,3,64,128]{3,2,1,0:T(8,128)(2,1)S(1)}, u32[]{:S(2)}, u32[]{:S(2)}) async-start(bf16[8,3,64,128]{3,2,1,0:T(8,128)(2,1)} %bitcast.11), calls=%async_computation.1 | async-start | bytes 786432 | tf_op jit(solution)/shard_map/all_to_all | solution.py:125
  69.4 3.8 %collective-permute-start.5 = (bf16[1,3,64,128]{3,2,1,0:T(8,128)(2,1)S(1)}, bf16[1,3,64,128]{3,2,1,0:T(8,128)(2,1)S(1)}, u32[]{:S(2)}, u32[]{:S(2)}) collective-permute-start(bf16[1,3,64,128]{3,2,1,0:T(8,128)(2,1)S(1)} %get-tuple-element.73), channel_id=1, source_target_pairs={{0,12},{2,14},{4,8},{6,10},{8,4},{10,6},{12,0},{14,2},{1,13},{3,15... | collective-permute-start | bytes 147464 | tf_op jit(solution)/shard_map/ppermute | solution.py:29
  73.4 7.9 %collective-permute-done.5 = bf16[1,3,64,128]{3,2,1,0:T(8,128)(2,1)S(1)} collective-permute-done((bf16[1,3,64,128]{3,2,1,0:T(8,128)(2,1)S(1)}, bf16[1,3,64,128]{3,2,1,0:T(8,128)(2,1)S(1)}, u32[]{:S(2)}, u32[]{:S(2)}) %collective-permute-start.5) | collective-permute-done | bytes 49184 | tf_op jit(solution)/shard_map/ppermute | solution.py:29
  82.1 1.4 %all-to-all-done.1 = bf16[8,3,64,128]{3,2,1,0:T(8,128)(2,1)S(1)} async-done(((bf16[8,3,64,128]{3,2,1,0:T(8,128)(2,1)}), bf16[8,3,64,128]{3,2,1,0:T(8,128)(2,1)S(1)}, u32[]{:S(2)}, u32[]{:S(2)}) %all-to-all-start.1) | async-done | bytes 393248 | tf_op jit(solution)/shard_map/all_to_all | solution.py:125
  84.8 1.2 slice.60
  85.9 1.7 %fusion.21 = (f32[1536,128]{1,0:T(8,128)S(1)}, f32[1536,128]{1,0:T(8,128)S(1)}) fusion(f32[24,64,128]{2,1,0:T(8,128)S(1)} %get-tuple-element.69, f32[1536]{0:T(1024)S(1)} %mul.126, f32[1536]{0:T(1024)S(1)} %mul.122, f32[1536]{0:T(1024)S(1)} %mul.119, bf16[8,3,64,128]{3,2,1,0:T(8,128)(2,1)S(1)} %gather_fusion, f32[1536,1]{1,0:T(8,128)S(1)} %bitcast.133, ...), kind=kLoop, calls=%fused_computation.38 | loop fusion | flops 3145728 | bytes 4744704 | tf_op jit(solution)/shard_map/mul | solution.py:87
  87.6 10.6 %scatter_custom_fusion.3 = f32[512,128]{1,0:T(8,128)} fusion(s32[1536]{0:T(1024)S(1)} %fusion.32, f32[1536,128]{1,0:T(8,128)S(1)} %get-tuple-element.81, f32[1536,128]{1,0:T(8,128)S(1)} %get-tuple-element.80, f32[1536,1]{1,0:T(8,128)} %bitcast.135, f32[]{:T(128)} %constant.77, f32[1536,127]{1,0:T(8,128)S(1)} %bitcast.134, f32[1536]{0:T(1024)S(1)} %mul.131, ...), kind=kCustom, calls=%fused_computation.33 | custom fusion | flops 983040 | bytes 2635784 | tf_op jit(solution)/shard_map/scatter-add | solution.py:138
  98.3 9.4 %scatter_custom_fusion.4 = f32[512,128]{1,0:T(8,128)} fusion(s32[1536]{0:T(1024)S(1)} %fusion.32, f32[1536,128]{1,0:T(8,128)S(1)} %get-tuple-element.81, f32[]{:T(128)} %constant.26.clone.1), kind=kCustom, calls=%fused_computation.49 | custom fusion | flops 196608 | bytes 262148 | tf_op jit(solution)/shard_map/scatter-add | solution.py:143
  107.7 2.8 %reduce-scatter.3.cloned.1.call-done = f32[256,128]{1,0:T(8,128)} async-done(((f32[512,128]{1,0:T(8,128)}), f32[256,128]{1,0:T(8,128)}) %reduce-scatter.3.cloned.1.call-update) | async-done | bytes 131088 | tf_op jit(solution)/shard_map/reduce_scatter | solution.py:146
  110.5 14.0 %reduce-scatter.5.cloned.1.call-done = f32[256,128]{1,0:T(8,128)} async-done(((f32[512,128]{1,0:T(8,128)}), f32[256,128]{1,0:T(8,128)}) %reduce-scatter.5.cloned.1.call-update) | async-done | bytes 131088 | tf_op jit(solution)/shard_map/reduce_scatter | solution.py:147
  124.5 1.6 %add_divide_fusion = f32[256,128]{1,0:T(8,128)} fusion(f32[256,128]{1,0:T(8,128)} %reduce-scatter.3.cloned.1.call-done, f32[256,128]{1,0:T(8,128)} %reduce-scatter.5.cloned.1.call-done), kind=kLoop, calls=%fused_computation.48 | loop fusion | flops 65536 | bytes 393216 | tf_op jit(solution)/shard_map/div | solution.py:149
  (97 shorter events, 7.9 us)
Async XLA Ops:
  6.5 6.6 %copy-start = (f32[400,21]{0,1:T(8,128)S(1)}, f32[400,21]{0,1:T(8,128)}, u32[]{:S(2)}) copy-start(f32[400,21]{0,1:T(8,128)} %param.15) | copy-start | bytes 100804
  10.3 1.7 %copy-start.4 = (bf16[21,41]{1,0:T(8,128)(2,1)S(1)}, bf16[21,41]{1,0:T(8,128)(2,1)}, u32[]{:S(2)}) copy-start(bf16[21,41]{1,0:T(8,128)(2,1)} %param.13) | copy-start | bytes 5170
  10.8 2.4 %copy-start.5 = (s32[24]{0:T(128)S(1)}, s32[24]{0:T(128)}, u32[]{:S(2)}) copy-start(s32[24]{0:T(128)} %param.16) | copy-start | bytes 292
  43.7 7.8 %copy-start.2 = (s32[24,2]{0,1:T(2,128)S(1)}, s32[24,2]{0,1:T(2,128)}, u32[]{:S(2)}) copy-start(s32[24,2]{0,1:T(2,128)} %param.19) | copy-start | bytes 580
  43.7 7.8 %copy-start.3 = (s32[24]{0:T(128)S(1)}, s32[24]{0:T(128)}, u32[]{:S(2)}) copy-start(s32[24]{0:T(128)} %param.18) | copy-start | bytes 292
  43.7 15.1 %copy-start.1 = (bf16[24,64,128]{2,1,0:T(8,128)(2,1)S(1)}, bf16[24,64,128]{2,1,0:T(8,128)(2,1)}, u32[]{:S(2)}) copy-start(bf16[24,64,128]{2,1,0:T(8,128)(2,1)} %param.12) | copy-start | bytes 1179652
  45.5 23.9 %collective-permute-start = (bf16[1,3,64,128]{3,2,1,0:T(8,128)(2,1)S(1)}, bf16[1,3,64,128]{3,2,1,0:T(8,128)(2,1)S(1)}, u32[]{:S(2)}, u32[]{:S(2)}) collective-permute-start(bf16[1,3,64,128]{3,2,1,0:T(8,128)(2,1)S(1)} %get-tuple-element.78), channel_id=1, source_target_pairs={{0,2},{2,0},{4,6},{6,4},{8,10},{10,8},{12,14},{14,12},{1,3},{3,1},... | collective-permute-start | bytes 147464 | tf_op jit(solution)/shard_map/ppermute | solution.py:29
  46.0 27.2 %collective-permute-start.1 = (bf16[1,3,64,128]{3,2,1,0:T(8,128)(2,1)S(1)}, bf16[1,3,64,128]{3,2,1,0:T(8,128)(2,1)S(1)}, u32[]{:S(2)}, u32[]{:S(2)}) collective-permute-start(bf16[1,3,64,128]{3,2,1,0:T(8,128)(2,1)S(1)} %get-tuple-element.77), channel_id=1, source_target_pairs={{0,4},{2,6},{4,0},{6,2},{8,12},{10,14},{12,8},{14,10},{1,5},{3,7},... | collective-permute-start | bytes 147464 | tf_op jit(solution)/shard_map/ppermute | solution.py:29
  48.7 24.7 %collective-permute-start.2 = (bf16[1,3,64,128]{3,2,1,0:T(8,128)(2,1)S(1)}, bf16[1,3,64,128]{3,2,1,0:T(8,128)(2,1)S(1)}, u32[]{:S(2)}, u32[]{:S(2)}) collective-permute-start(bf16[1,3,64,128]{3,2,1,0:T(8,128)(2,1)S(1)} %get-tuple-element.76), channel_id=1, source_target_pairs={{0,6},{2,4},{4,2},{6,0},{8,14},{10,12},{12,10},{14,8},{1,7},{3,5},... | collective-permute-start | bytes 147464 | tf_op jit(solution)/shard_map/ppermute | solution.py:29
  48.7 24.7 %collective-permute-start.3 = (bf16[1,3,64,128]{3,2,1,0:T(8,128)(2,1)S(1)}, bf16[1,3,64,128]{3,2,1,0:T(8,128)(2,1)S(1)}, u32[]{:S(2)}, u32[]{:S(2)}) collective-permute-start(bf16[1,3,64,128]{3,2,1,0:T(8,128)(2,1)S(1)} %get-tuple-element.75), channel_id=1, source_target_pairs={{0,8},{2,10},{4,12},{6,14},{8,0},{10,2},{12,4},{14,6},{1,9},{3,11}... | collective-permute-start | bytes 147464 | tf_op jit(solution)/shard_map/ppermute | solution.py:29
  51.5 21.9 %collective-permute-start.4 = (bf16[1,3,64,128]{3,2,1,0:T(8,128)(2,1)S(1)}, bf16[1,3,64,128]{3,2,1,0:T(8,128)(2,1)S(1)}, u32[]{:S(2)}, u32[]{:S(2)}) collective-permute-start(bf16[1,3,64,128]{3,2,1,0:T(8,128)(2,1)S(1)} %get-tuple-element.74), channel_id=1, source_target_pairs={{0,10},{2,8},{4,14},{6,12},{8,2},{10,0},{12,6},{14,4},{1,11},{3,9}... | collective-permute-start | bytes 147464 | tf_op jit(solution)/shard_map/ppermute | solution.py:29
  53.1 10.6 %all-to-all-start = ((s32[8,3,4]{1,2,0:T(4,128)}), s32[8,3,4]{1,2,0:T(4,128)S(1)}, u32[]{:S(2)}, u32[]{:S(2)}) async-start(s32[8,3,4]{1,2,0:T(4,128)} %copy.32), calls=%async_computation | async-start | bytes 32768 | tf_op jit(solution)/shard_map/all_to_all | solution.py:126
  63.6 19.8 %all-to-all-start.1 = ((bf16[8,3,64,128]{3,2,1,0:T(8,128)(2,1)}), bf16[8,3,64,128]{3,2,1,0:T(8,128)(2,1)S(1)}, u32[]{:S(2)}, u32[]{:S(2)}) async-start(bf16[8,3,64,128]{3,2,1,0:T(8,128)(2,1)} %bitcast.11), calls=%async_computation.1 | async-start | bytes 786432 | tf_op jit(solution)/shard_map/all_to_all | solution.py:125
  68.3 42.2 %reduce-scatter.3.cloned.1.call-start = ((), (), s32[]{:S(2)}) async-start(), calls=%async_computation.4 | async-start | bytes 393216 | tf_op jit(solution)/shard_map/reduce_scatter | solution.py:146
  69.4 11.9 %collective-permute-start.5 = (bf16[1,3,64,128]{3,2,1,0:T(8,128)(2,1)S(1)}, bf16[1,3,64,128]{3,2,1,0:T(8,128)(2,1)S(1)}, u32[]{:S(2)}, u32[]{:S(2)}) collective-permute-start(bf16[1,3,64,128]{3,2,1,0:T(8,128)(2,1)S(1)} %get-tuple-element.73), channel_id=1, source_target_pairs={{0,12},{2,14},{4,8},{6,10},{8,4},{10,6},{12,0},{14,2},{1,13},{3,15... | collective-permute-start | bytes 147464 | tf_op jit(solution)/shard_map/ppermute | solution.py:29
  73.2 8.1 %collective-permute-start.6 = (bf16[1,3,64,128]{3,2,1,0:T(8,128)(2,1)S(1)}, bf16[1,3,64,128]{3,2,1,0:T(8,128)(2,1)S(1)}, u32[]{:S(2)}, u32[]{:S(2)}) collective-permute-start(bf16[1,3,64,128]{3,2,1,0:T(8,128)(2,1)S(1)} %get-tuple-element.72), channel_id=1, source_target_pairs={{0,14},{2,12},{4,10},{6,8},{8,6},{10,4},{12,2},{14,0},{1,15},{3,13... | collective-permute-start | bytes 147464 | tf_op jit(solution)/shard_map/ppermute | solution.py:29
  98.3 26.2 %reduce-scatter.5.cloned.1.call-start = ((), (), s32[]{:S(2)}) async-start(), calls=%async_computation.5 | async-start | bytes 393216 | tf_op jit(solution)/shard_map/reduce_scatter | solution.py:147
Sparse Core Ops, SparseCore 0:
  98.4 12.0 reduce-scatter.2
  112.7 11.7 reduce-scatter.4
